TPU v7x, 32 devices: a whole 2x2x4 slice. The times are simulated.
32 devices in a mesh: fsdp: 4 (over y, core), ctx: 8 (over z, x).
Axes of the slice: x: 2, y: 2, z: 4, core: 2. Of those that a mesh axis runs over, the one named last changes fastest.
Arguments:
- query_proj: bfloat16 [4, 1024, 4096], P('fsdp', 'ctx'), may hold values from -10 to 10
- key_proj: bfloat16 [4, 1024, 4096], P('fsdp', 'ctx'), may hold values from -10 to 10
- value_proj: bfloat16 [4, 1024, 4096], P('fsdp', 'ctx'), may hold values from -12 to 12
- modality: int32 [4, 1024], P('fsdp', 'ctx'), may hold values from 0 to 1, as said below
- out_weight: bfloat16 [2, 4096, 2048], P(None, ('fsdp', 'ctx')), may hold values from -0.09375 to 0.09375
- grad_projected: bfloat16 [4, 1024, 2048], P('fsdp', 'ctx'), may hold values from -6 to 6
Outputs:
- projected: bfloat16 [4, 1024, 2048], P('fsdp', 'ctx')
- grad_query: bfloat16 [4, 1024, 4096], P('fsdp', 'ctx')
- grad_key: bfloat16 [4, 1024, 4096], P('fsdp', 'ctx')
- grad_value: bfloat16 [4, 1024, 4096], P('fsdp', 'ctx')
Inputs may be any that keep to these rules, and one draw needn't show every extreme that they name: `modality`: each sequence holds exactly two image spans of 256 positions each, one starting within the first half and lying in the first half, the other lying in the second half; all other positions are text, so exactly half of each sequence's positions are image.
All inputs are finite; a program needn't handle non-finite values.
Results may differ from a plain program's by a relative error of at most 0.012.
The roundings to bfloat16 on the way count: a program that leaves them out, or rounds other values in their place, can miss the bound.
Values may be sent and summed in bfloat16 or wider, within the bound.
A program may use at most 320 MiB of HBM per device.

v0:
```python
import jax
import jax.numpy as jnp
from jax import lax
from jax.sharding import PartitionSpec as P

HEAD_SIZE = 128


def block_count(length):
    return max(1, min(8, length // 512))


def probabilities(query_block, key_prefix, offset):
    scaling = query_block.shape[-1] ** (-0.5)
    scores = (
        jnp.einsum("hqd,hkd->hqk", query_block, key_prefix, preferred_element_type=jnp.float32)
        * scaling
    )
    query_places = offset + jnp.arange(query_block.shape[1])
    key_places = jnp.arange(key_prefix.shape[1])
    scores = jnp.where(key_places[None, None, :] <= query_places[None, :, None], scores, -jnp.inf)
    highest = jnp.max(scores, axis=-1, keepdims=True)
    raised = jnp.exp(scores - highest)
    return raised / jnp.sum(raised, axis=-1, keepdims=True)


def attend_forward(queries, keys_all, values_all):
    length = queries.shape[1]
    block_rows = length // block_count(length)
    pieces = []
    for block_index in range(length // block_rows):
        offset = block_index * block_rows
        finish = offset + block_rows
        weights = probabilities(queries[:, offset:finish], keys_all[:, :finish], offset).astype(
            jnp.bfloat16
        )
        output = jnp.einsum(
            "hqk,hkd->hqd", weights, values_all[:, :finish], preferred_element_type=jnp.float32
        )
        pieces.append(output.astype(jnp.bfloat16))
    return jnp.concatenate(pieces, axis=1)


def attend_backward(queries, keys_all, values_all, attention, grad_attention):
    length = queries.shape[1]
    block_rows = length // block_count(length)
    scaling = queries.shape[-1] ** (-0.5)
    grad_keys = jnp.zeros(queries.shape, jnp.float32)
    grad_values = jnp.zeros(queries.shape, jnp.float32)
    query_pieces = []
    for block_index in range(length // block_rows):
        offset = block_index * block_rows
        finish = offset + block_rows
        query_block = queries[:, offset:finish]
        weights = probabilities(query_block, keys_all[:, :finish], offset)
        grad_block = grad_attention[:, offset:finish]
        attn_block = attention[:, offset:finish]
        grad_values = grad_values.at[:, :finish].add(
            jnp.einsum(
                "hqk,hqd->hkd",
                weights.astype(jnp.bfloat16),
                grad_block,
                preferred_element_type=jnp.float32,
            )
        )
        grad_weights = jnp.einsum(
            "hqd,hkd->hqk", grad_block, values_all[:, :finish], preferred_element_type=jnp.float32
        )
        row_delta = jnp.sum(
            grad_block.astype(jnp.float32) * attn_block.astype(jnp.float32), axis=-1, keepdims=True
        )
        grad_scores = (weights * (grad_weights - row_delta) * scaling).astype(jnp.bfloat16)
        query_pieces.append(
            jnp.einsum(
                "hqk,hkd->hqd",
                grad_scores,
                keys_all[:, :finish],
                preferred_element_type=jnp.float32,
            ).astype(jnp.bfloat16)
        )
        grad_keys = grad_keys.at[:, :finish].add(
            jnp.einsum("hqk,hqd->hkd", grad_scores, query_block, preferred_element_type=jnp.float32)
        )
    return (
        jnp.concatenate(query_pieces, axis=1),
        grad_keys.astype(jnp.bfloat16),
        grad_values.astype(jnp.bfloat16),
    )


def transposed_product(left, right):
    return lax.dot_general(
        left, right, (((1,), (1,)), ((), ())), preferred_element_type=jnp.float32
    )


def heads_first(flat, length, local_heads):
    return flat.reshape(length, local_heads, HEAD_SIZE).transpose(1, 0, 2)


def heads_last(stacked, length, local_width):
    return stacked.transpose(1, 0, 2).reshape(1, length, local_width)


def per_device(query_proj, key_proj, value_proj, modality, out_weight, grad_projected):
    context_size = lax.axis_size("ctx")
    row_count = query_proj.shape[1]
    inner_width = query_proj.shape[2]
    length = row_count * context_size
    local_width = inner_width // context_size
    local_heads = local_width // HEAD_SIZE
    head_query, head_key, head_value = (
        lax.all_to_all(query_proj, "ctx", split_axis=2, concat_axis=1, tiled=True),
        lax.all_to_all(key_proj, "ctx", split_axis=2, concat_axis=1, tiled=True),
        lax.all_to_all(value_proj, "ctx", split_axis=2, concat_axis=1, tiled=True),
    )
    head_query = heads_first(head_query, length, local_heads)
    head_key = heads_first(head_key, length, local_heads)
    head_value = heads_first(head_value, length, local_heads)
    attention = attend_forward(head_query, head_key, head_value)
    sending = heads_last(attention, length, local_width)
    attn_rows = lax.all_to_all(sending, "ctx", split_axis=1, concat_axis=2, tiled=True)[0]
    upstream = grad_projected[0]
    weight_piece = lax.all_gather(out_weight, ("fsdp", "ctx"), axis=1, tiled=True)
    text_out = jnp.dot(attn_rows, weight_piece[0], preferred_element_type=jnp.float32)
    image_out = jnp.dot(attn_rows, weight_piece[1], preferred_element_type=jnp.float32)
    text_grad = transposed_product(upstream, weight_piece[0])
    image_grad = transposed_product(upstream, weight_piece[1])
    text_out, image_out, text_grad, image_grad = (text_out, image_out, text_grad, image_grad)
    image_rows = (modality[0] == 1)[:, None]
    projected = jnp.where(image_rows, image_out, text_out).astype(jnp.bfloat16)[None]
    grad_rows = jnp.where(image_rows, image_grad, text_grad).astype(jnp.bfloat16)
    grad_heads = lax.all_to_all(grad_rows[None], "ctx", split_axis=2, concat_axis=1, tiled=True)
    grad_heads = heads_first(grad_heads, length, local_heads)
    grad_q, grad_k, grad_v = attend_backward(
        head_query, head_key, head_value, attention, grad_heads
    )
    grad_query, grad_key, grad_value = (
        lax.all_to_all(
            heads_last(grad_q, length, local_width), "ctx", split_axis=1, concat_axis=2, tiled=True
        ),
        lax.all_to_all(
            heads_last(grad_k, length, local_width), "ctx", split_axis=1, concat_axis=2, tiled=True
        ),
        lax.all_to_all(
            heads_last(grad_v, length, local_width), "ctx", split_axis=1, concat_axis=2, tiled=True
        ),
    )
    return (projected, grad_query, grad_key, grad_value)


def solution(mesh):
    placed = (
        P("fsdp", "ctx", None),
        P("fsdp", "ctx", None),
        P("fsdp", "ctx", None),
        P("fsdp", "ctx"),
        P(None, ("fsdp", "ctx"), None),
        P("fsdp", "ctx", None),
    )
    return jax.shard_map(
        per_device,
        mesh=mesh,
        in_specs=placed,
        out_specs=(
            P("fsdp", "ctx", None),
            P("fsdp", "ctx", None),
            P("fsdp", "ctx", None),
            P("fsdp", "ctx", None),
        ),
        check_vma=False,
    )
```

profile of v0, /device:TPU:0, one launch (start us, length us, event | category | flops | bytes accessed | tf_op | source)
XLA Modules:
  0.0 543.5 jit_solution(6970841541703421704)
XLA Ops:
  7.9 5.0 copy.130
  13.5 23.4 %reduce.8 = bf16[4096,128]{1,0:T(8,128)(2,1)} reduce(bf16[4096,1,128]{2,1,0:T(2,128)(2,1)S(1)} %bitcast.141, bf16[]{:T(256)} %broadcast.182), dimensions={1}, to_apply=%bitcast.103.reduce_sub_computation | reduce | bytes 2097154
  39.0 7.3 %all-to-all-start = ((bf16[8,2,32768]{2,1,0:T(2,128)(2,1)}), bf16[8,2,32768]{2,1,0:T(2,128)(2,1)}, u32[]{:S(2)}, u32[]{:S(2)}) async-start(bf16[8,2,32768]{2,1,0:T(2,128)(2,1)} %reshape.224), calls=%async_computation | async-start | bytes 2097152 | tf_op jit(solution)/shard_map/all_to_all | solution.py:113
  46.2 5.0 copy.133
  51.3 23.4 %reduce.9 = bf16[4096,128]{1,0:T(8,128)(2,1)} reduce(bf16[4096,1,128]{2,1,0:T(2,128)(2,1)S(1)} %bitcast.147, bf16[]{:T(256)} %broadcast.182), dimensions={1}, to_apply=%bitcast.105.reduce_sub_computation | reduce | bytes 2097154
  76.8 16.4 %all-to-all-done = bf16[8,2,32768]{2,1,0:T(2,128)(2,1)} async-done(((bf16[8,2,32768]{2,1,0:T(2,128)(2,1)}), bf16[8,2,32768]{2,1,0:T(2,128)(2,1)}, u32[]{:S(2)}, u32[]{:S(2)}) %all-to-all-start) | async-done | bytes 1048608 | tf_op jit(solution)/shard_map/all_to_all | solution.py:113
  93.2 7.5 %all-to-all-start.1 = ((bf16[8,2,32768]{2,1,0:T(2,128)(2,1)}), bf16[8,2,32768]{2,1,0:T(2,128)(2,1)}, u32[]{:S(2)}, u32[]{:S(2)}) async-start(bf16[8,2,32768]{2,1,0:T(2,128)(2,1)} %reshape.226), calls=%async_computation.1 | async-start | bytes 2097152 | tf_op jit(solution)/shard_map/all_to_all | solution.py:114
  100.7 5.0 copy.136
  105.7 23.4 %reduce.10 = bf16[4096,128]{1,0:T(8,128)(2,1)} reduce(bf16[4096,1,128]{2,1,0:T(2,128)(2,1)S(1)} %bitcast.148, bf16[]{:T(256)} %broadcast.182), dimensions={1}, to_apply=%bitcast.107.reduce_sub_computation | reduce | bytes 2097154
  139.9 5.2 all-to-all-start.2
  153.3 5.2 fusion.58
  158.5 103.3 %all-gather.2.cloned.1.call-done = bf16[2,4096,2048]{2,1,0:T(8,128)(2,1)} async-done(((bf16[2,128,2048]{2,1,0:T(8,128)(2,1)}), bf16[2,4096,2048]{2,1,0:T(8,128)(2,1)}) %all-gather.2.cloned.1.call-update) | async-done | bytes 33554448 | tf_op jit(solution)/shard_map/all_gather | solution.py:124
  261.9 11.4 %fusion.2 = bf16[128,4096]{1,0:T(8,128)(2,1)S(1)} fusion(bf16[2,4096,2048]{2,1,0:T(8,128)(2,1)} %all-gather.2.cloned.1.call-done, bf16[1,128,2048]{2,1,0:T(8,128)(2,1)S(1)} %copy-done), kind=kOutput, calls=%fused_computation.4 | convolution fusion | flops 2147483648 | bytes 18350080 | tf_op jit(solution)/shard_map/dot_general | solution.py:92
  273.2 12.3 %fusion.9 = bf16[1,128,4096]{2,1,0:T(8,128)(2,1)} fusion(bf16[128,4096]{1,0:T(8,128)(2,1)S(1)} %fusion.2, bf16[2,4096,2048]{2,1,0:T(8,128)(2,1)} %all-gather.2.cloned.1.call-done, pred[128]{0:T(512)(128)(4,1)S(1)} %compare_bitcast_fusion, bf16[1,128,2048]{2,1,0:T(8,128)(2,1)S(1)} %copy-done), kind=kOutput, calls=%fused_computation.14 | convolution fusion | flops 2148007936 | bytes 19398784 | tf_op jit(solution)/shard_map/dot_general | solution.py:92
  285.6 5.0 copy.143
  290.6 23.5 %reduce.11 = bf16[4096,128]{1,0:T(8,128)(2,1)} reduce(bf16[4096,1,128]{2,1,0:T(2,128)(2,1)S(1)} %bitcast.143, bf16[]{:T(256)} %broadcast.182), dimensions={1}, to_apply=%bitcast.111.reduce_sub_computation | reduce | bytes 2097154
  320.6 5.3 fusion.13
  347.0 5.8 %reshape.233 = bf16[4096,1,128]{2,1,0:T(2,128)(2,1)} reshape(bf16[8,2,32768]{2,1,0:T(2,128)(2,1)} %all-to-all-done.4) | data formatting | bytes 2097152
  368.9 6.1 %copy.141 = bf16[1,1024,512]{2,0,1:T(2,128)(2,1)} copy(bf16[1,1024,512]{1,2,0:T(8,128)(2,1)} %bitcast.157) | data formatting | bytes 2097152 | tf_op jit(solution)/shard_map/reshape | solution.py:102
  375.0 9.0 %reduce.12 = bf16[1024,512]{1,0:T(8,128)(2,1)} reduce(bf16[1024,1,512]{2,1,0:T(2,128)(2,1)} %bitcast.144, bf16[]{:T(256)} %broadcast.182), dimensions={1}, to_apply=%bitcast.109.reduce_sub_computation | reduce | bytes 2097154
  386.7 4.6 all-to-all-start.3
  393.2 5.5 %multiply_convert_fusion = bf16[4,512,1024]{2,1,0:T(8,128)(2,1)S(1)} fusion(f32[4,512]{1,0:T(4,128)S(1)} %get-tuple-element.85, f32[4,512,1024]{2,1,0:T(8,128)} %get-tuple-element.87, f32[4,512]{1,0:T(4,128)S(1)} %get-tuple-element.86, bf16[4,1024,128]{2,1,0:T(8,128)(2,1)} %bitcast.172, bf16[1024,4,128]{2,0,1:T(8,128)(2,1)} %copy.138), kind=kOutput, calls=%fused_computation.8 | convolution fusion | flops 547356672 | bytes 14172160 | tf_op jit(solution)/shard_map/hqd,hkd->hqk/dot_general | solution.py:66
  401.0 6.0 %copy.154 = bf16[1,1024,512]{2,0,1:T(2,128)(2,1)} copy(bf16[1,1024,512]{1,2,0:T(8,128)(2,1)} %bitcast.166) | data formatting | bytes 2097152 | tf_op jit(solution)/shard_map/reshape | solution.py:102
  407.0 9.0 %reduce.14 = bf16[1024,512]{1,0:T(8,128)(2,1)} reduce(bf16[1024,1,512]{2,1,0:T(2,128)(2,1)} %bitcast.145, bf16[]{:T(256)} %broadcast.182), dimensions={1}, to_apply=%bitcast.115.reduce_sub_computation | reduce | bytes 2097154
  418.6 6.2 %all-to-all-start.6 = ((bf16[8,2,32768]{2,1,0:T(2,128)(2,1)}), bf16[8,2,32768]{2,1,0:T(2,128)(2,1)}, u32[]{:S(2)}, u32[]{:S(2)}) async-start(bf16[8,2,32768]{2,1,0:T(2,128)(2,1)} %reshape.236), calls=%async_computation.6 | async-start | bytes 2097152 | tf_op jit(solution)/shard_map/all_to_all | solution.py:142
  435.0 9.2 %reduce.13 = bf16[1024,512]{1,0:T(8,128)(2,1)} reduce(bf16[1024,1,512]{2,1,0:T(2,128)(2,1)} %bitcast.146, bf16[]{:T(256)} %broadcast.182), dimensions={1}, to_apply=%bitcast.113.reduce_sub_computation | reduce | bytes 2097154
  450.3 4.5 all-to-all-start.5
  460.8 4.6 copy.159
  465.4 8.0 %reduce.15 = bf16[1024,512]{1,0:T(8,128)(2,1)} reduce(bf16[1024,1,512]{2,1,0:T(2,128)(2,1)S(1)} %bitcast.142, bf16[]{:T(256)} %broadcast.182), dimensions={1}, to_apply=%bitcast.117.reduce_sub_computation | reduce | bytes 2097154
  480.2 4.5 all-to-all-start.7
  518.6 8.5 %fusion.3 = bf16[128,2048]{1,0:T(8,128)(2,1)S(1)} fusion(bf16[128,4096]{0,1:T(8,128)(2,1)} %bitcast.177, bf16[2,4096,2048]{2,1,0:T(8,128)(2,1)} %all-gather.2.cloned.1.call-done), kind=kOutput, calls=%fused_computation.5 | convolution fusion | flops 2147483648 | bytes 18350080 | tf_op jit(solution)/shard_map/dot_general | solution.py:126
  527.2 9.0 %fusion.17 = bf16[1,128,2048]{2,1,0:T(8,128)(2,1)} fusion(bf16[128,2048]{1,0:T(8,128)(2,1)S(1)} %fusion.3, bf16[128,4096]{0,1:T(8,128)(2,1)S(1)} %bitcast.178, bf16[2,4096,2048]{2,1,0:T(8,128)(2,1)} %all-gather.2.cloned.1.call-done, pred[128]{0:T(512)(128)(4,1)S(1)} %compare_bitcast_fusion), kind=kOutput, calls=%fused_computation.26 | convolution fusion | flops 2147745792 | bytes 18874496 | tf_op jit(solution)/shard_map/dot_general | solution.py:125
  (106 shorter events, 140.3 us)
Async XLA Ops:
  7.2 254.7 %copy-start = (bf16[1,128,2048]{2,1,0:T(8,128)(2,1)S(1)}, bf16[1,128,2048]{2,1,0:T(8,128)(2,1)}, u32[]{:S(2)}) copy-start(bf16[1,128,2048]{2,1,0:T(8,128)(2,1)} %param.23) | copy-start | bytes 1572868
  7.2 254.7 %all-gather.2.cloned.1.call-start = ((), (), s32[]{:S(2)}) async-start(), calls=%async_computation.8 | async-start | bytes 34603008 | tf_op jit(solution)/shard_map/all_gather | solution.py:124
  39.0 54.2 %all-to-all-start = ((bf16[8,2,32768]{2,1,0:T(2,128)(2,1)}), bf16[8,2,32768]{2,1,0:T(2,128)(2,1)}, u32[]{:S(2)}, u32[]{:S(2)}) async-start(bf16[8,2,32768]{2,1,0:T(2,128)(2,1)} %reshape.224), calls=%async_computation | async-start | bytes 2097152 | tf_op jit(solution)/shard_map/all_to_all | solution.py:113
  93.2 46.7 %all-to-all-start.1 = ((bf16[8,2,32768]{2,1,0:T(2,128)(2,1)}), bf16[8,2,32768]{2,1,0:T(2,128)(2,1)}, u32[]{:S(2)}, u32[]{:S(2)}) async-start(bf16[8,2,32768]{2,1,0:T(2,128)(2,1)} %reshape.226), calls=%async_computation.1 | async-start | bytes 2097152 | tf_op jit(solution)/shard_map/all_to_all | solution.py:114
  100.6 30.7 %copy-start.15 = (s32[1,128]{1,0:T(1,128)S(1)}, s32[1,128]{1,0:T(1,128)}, u32[]{:S(2)}) copy-start(s32[1,128]{1,0:T(1,128)} %param.21) | copy-start | bytes 1540
  139.9 176.4 %all-to-all-start.2 = ((bf16[8,2,32768]{2,1,0:T(2,128)(2,1)}), bf16[8,2,32768]{2,1,0:T(2,128)(2,1)}, u32[]{:S(2)}, u32[]{:S(2)}) async-start(bf16[8,2,32768]{2,1,0:T(2,128)(2,1)} %reshape.228), calls=%async_computation.2 | async-start | bytes 2097152 | tf_op jit(solution)/shard_map/all_to_all | solution.py:115
  149.7 3.6 copy-start.5
  153.3 5.3 copy-start.10
  316.3 30.7 %all-to-all-start.4 = ((bf16[8,2,32768]{2,1,0:T(2,128)(2,1)}), bf16[8,2,32768]{2,1,0:T(2,128)(2,1)}, u32[]{:S(2)}, u32[]{:S(2)}) async-start(bf16[8,2,32768]{2,1,0:T(2,128)(2,1)} %reshape.232), calls=%async_computation.4 | async-start | bytes 2097152 | tf_op jit(solution)/shard_map/all_to_all | solution.py:133
  330.4 6.2 %copy-start.6 = (bf16[1024,4,128]{2,0,1:T(8,128)(2,1)S(1)}, bf16[1024,4,128]{2,0,1:T(8,128)(2,1)}, u32[]{:S(2)}) copy-start(bf16[1024,4,128]{2,0,1:T(8,128)(2,1)} %copy.132) | copy-start | bytes 3145732
  330.4 6.2 %copy-start.11 = (bf16[1024,4,128]{2,0,1:T(8,128)(2,1)S(1)}, bf16[1024,4,128]{2,0,1:T(8,128)(2,1)}, u32[]{:S(2)}) copy-start(bf16[1024,4,128]{2,0,1:T(8,128)(2,1)} %copy-done.10) | copy-start | bytes 3145732
  336.6 2.2 copy-start.2
  336.6 2.5 copy-start.13
  342.5 1.9 copy-start.8
  345.1 15.7 %copy-start.3 = (bf16[4,512,512]{1,2,0:T(8,128)(2,1)}, bf16[4,512,512]{1,2,0:T(8,128)(2,1)S(1)}, u32[]{:S(2)}) copy-start(bf16[4,512,512]{1,2,0:T(8,128)(2,1)S(1)} %fusion.21) | copy-start | bytes 6291460
  360.7 2.8 copy-start.9
  386.7 31.9 %all-to-all-start.3 = ((bf16[8,2,32768]{2,1,0:T(2,128)(2,1)}), bf16[8,2,32768]{2,1,0:T(2,128)(2,1)}, u32[]{:S(2)}, u32[]{:S(2)}) async-start(bf16[8,2,32768]{2,1,0:T(2,128)(2,1)} %reshape.230), calls=%async_computation.3 | async-start | bytes 2097152 | tf_op jit(solution)/shard_map/all_to_all | solution.py:122
  393.2 5.5 %copy-start.7 = (bf16[1024,4,128]{2,0,1:T(8,128)(2,1)S(1)}, bf16[1024,4,128]{2,0,1:T(8,128)(2,1)}, u32[]{:S(2)}) copy-start(bf16[1024,4,128]{2,0,1:T(8,128)(2,1)} %copy.132) | copy-start | bytes 3145732
  398.7 2.3 copy-start.12
  418.6 31.8 %all-to-all-start.6 = ((bf16[8,2,32768]{2,1,0:T(2,128)(2,1)}), bf16[8,2,32768]{2,1,0:T(2,128)(2,1)}, u32[]{:S(2)}, u32[]{:S(2)}) async-start(bf16[8,2,32768]{2,1,0:T(2,128)(2,1)} %reshape.236), calls=%async_computation.6 | async-start | bytes 2097152 | tf_op jit(solution)/shard_map/all_to_all | solution.py:142
  435.0 19.8 %copy-start.4 = (bf16[4,512,512]{1,2,0:T(8,128)(2,1)S(1)}, bf16[4,512,512]{1,2,0:T(8,128)(2,1)}, u32[]{:S(2)}) copy-start(bf16[4,512,512]{1,2,0:T(8,128)(2,1)} %copy-done.3) | copy-start | bytes 6291460
  450.3 29.9 %all-to-all-start.5 = ((bf16[8,2,32768]{2,1,0:T(2,128)(2,1)}), bf16[8,2,32768]{2,1,0:T(2,128)(2,1)}, u32[]{:S(2)}, u32[]{:S(2)}) async-start(bf16[8,2,32768]{2,1,0:T(2,128)(2,1)} %reshape.234), calls=%async_computation.5 | async-start | bytes 2097152 | tf_op jit(solution)/shard_map/all_to_all | solution.py:139
  480.2 29.9 %all-to-all-start.7 = ((bf16[8,2,32768]{2,1,0:T(2,128)(2,1)}), bf16[8,2,32768]{2,1,0:T(2,128)(2,1)}, u32[]{:S(2)}, u32[]{:S(2)}) async-start(bf16[8,2,32768]{2,1,0:T(2,128)(2,1)} %reshape.238), calls=%async_computation.7 | async-start | bytes 2097152 | tf_op jit(solution)/shard_map/all_to_all | solution.py:145
  518.6 8.5 %copy-start.14 = (bf16[1,128,8,512]{1,3,2,0:T(8,128)(2,1)S(1)}, bf16[1,128,8,512]{1,3,2,0:T(8,128)(2,1)}, u32[]{:S(2)}) copy-start(bf16[1,128,8,512]{1,3,2,0:T(8,128)(2,1)} %copy.142) | copy-start | bytes 3145732
  527.2 9.1 %copy-start.1 = (bf16[1,128,2048]{2,1,0:T(8,128)(2,1)S(1)}, bf16[1,128,2048]{2,1,0:T(8,128)(2,1)}, u32[]{:S(2)}) copy-start(bf16[1,128,2048]{2,1,0:T(8,128)(2,1)} %param.23) | copy-start | bytes 1572868
Sparse Core Ops, SparseCore 0:
  11.0 250.7 all-gather.1
where the time goes:
time: 554 us; the launch traced here: 544 us
  local copies, waits for them, and re-layouts  140 us (25%)
  other arithmetic  139 us (25%)
  waiting for transfers between devices  132 us (24%)
  matrix products  74.5 us (13%)
  starting transfers between devices  44 us (8%)
  between operations  15 us (3%)
    unnamed x8, other arithmetic  129 us
    all_gather x1, waiting for transfers between devices, per_device(): lax.all_gather(out_weight, ('fsdp', 'ctx'), axis=1, tiled=True)  103 us
    unnamed x63, local copies, waits for them, and re-layouts  85.6 us
    dot_general x2, matrix products, transposed_product(): lax.dot_general(left, right, (((1,), (1,)), ((), ())), preferred_element_...  23.7 us
    reshape x4, local copies, waits for them, and re-layouts, heads_last(): return stacked.transpose(1, 0, 2).reshape(1, length, local_width)  20.6 us
    all_to_all x1, waiting for transfers between devices, per_device(): lax.all_to_all(query_proj, 'ctx', split_axis=2, concat_axis=1, tiled=True)  16.4 us
    reshape x8, local copies, waits for them, and re-layouts, heads_first(): return flat.reshape(length, local_heads, HEAD_SIZE).transpose(1, 0, 2)  13.8 us
  transfers between devices with their start and end apart: 9, of which 7 were waited for; matrix products, arithmetic and copies ran while one was open for 52% of the time, Pallas kernels for 0%

commit v1 on v0

--- a/solution.py
+++ b/solution.py
@@ -121,7 +121,7 @@
     sending = heads_last(attention, length, local_width)
     attn_rows = lax.all_to_all(sending, "ctx", split_axis=1, concat_axis=2, tiled=True)[0]
     upstream = grad_projected[0]
-    weight_piece = lax.all_gather(out_weight, ("fsdp", "ctx"), axis=1, tiled=True)
+    weight_piece = jnp.concatenate(lax.all_gather(out_weight, ("fsdp", "ctx")), axis=1)
     text_out = jnp.dot(attn_rows, weight_piece[0], preferred_element_type=jnp.float32)
     image_out = jnp.dot(attn_rows, weight_piece[1], preferred_element_type=jnp.float32)
     text_grad = transposed_product(upstream, weight_piece[0])

time: 554 us -> 579 us (1.045)
  local copies, waits for them, and re-layouts: 140 us -> 168 us
    slice x0 -> x1, local copies, waits for them, and re-layouts: none -> 23.6 us  [per_device(): weight_piece[0]]
    unnamed x63 -> x61, local copies, waits for them, and re-layouts: 85.6 us -> 91.8 us
  transfers between devices with their start and end apart: 9 -> 9, of which waited for: 7 -> 5; matrix products, arithmetic and copies ran while one was open for 52% -> 58% of each run, Pallas kernels for 0% -> 0%
where the time goes in v1:
time: 579 us; the launch traced here: 568 us
  local copies, waits for them, and re-layouts  168 us (29%)
  other arithmetic  139 us (24%)
  waiting for transfers between devices  127 us (22%)
  matrix products  73.9 us (13%)
  starting transfers between devices  46 us (8%)
  between operations  15 us (3%)
    unnamed x8, other arithmetic  129 us
    all_gather x1, waiting for transfers between devices, per_device(): lax.all_gather(out_weight, ('fsdp', 'ctx'))  103 us
    unnamed x61, local copies, waits for them, and re-layouts  91.8 us
    dot_general x2, matrix products, transposed_product(): lax.dot_general(left, right, (((1,), (1,)), ((), ())), preferred_element_...  23.7 us
    slice x1, local copies, waits for them, and re-layouts, per_device(): weight_piece[0]  23.6 us
    reshape x4, local copies, waits for them, and re-layouts, heads_last(): return stacked.transpose(1, 0, 2).reshape(1, length, local_width)  20.7 us
    all_to_all x1, waiting for transfers between devices, per_device(): lax.all_to_all(query_proj, 'ctx', split_axis=2, concat_axis=1, tiled=True)  16.3 us
    reshape x8, local copies, waits for them, and re-layouts, heads_first(): return flat.reshape(length, local_heads, HEAD_SIZE).transpose(1, 0, 2)  13.8 us
  transfers between devices with their start and end apart: 9, of which 5 were waited for; matrix products, arithmetic and copies ran while one was open for 58% of the time, Pallas kernels for 0%

profile of v1, /device:TPU:0, one launch (start us, length us, event | category | flops | bytes accessed | tf_op | source)
XLA Modules:
  0.0 568.4 jit_solution(203485944951900923)
XLA Ops:
  7.9 5.0 copy.130
  13.5 23.4 %reduce.8 = bf16[4096,128]{1,0:T(8,128)(2,1)} reduce(bf16[4096,1,128]{2,1,0:T(2,128)(2,1)S(1)} %bitcast.137, bf16[]{:T(256)} %broadcast.182), dimensions={1}, to_apply=%bitcast.88.reduce_sub_computation | reduce | bytes 2097154
  39.0 7.3 %all-to-all-start = ((bf16[8,2,32768]{2,1,0:T(2,128)(2,1)}), bf16[8,2,32768]{2,1,0:T(2,128)(2,1)}, u32[]{:S(2)}, u32[]{:S(2)}) async-start(bf16[8,2,32768]{2,1,0:T(2,128)(2,1)} %reshape.234), calls=%async_computation | async-start | bytes 2097152 | tf_op jit(solution)/shard_map/all_to_all | solution.py:113
  46.2 5.0 copy.133
  51.3 23.4 %reduce.9 = bf16[4096,128]{1,0:T(8,128)(2,1)} reduce(bf16[4096,1,128]{2,1,0:T(2,128)(2,1)S(1)} %bitcast.143, bf16[]{:T(256)} %broadcast.182), dimensions={1}, to_apply=%bitcast.90.reduce_sub_computation | reduce | bytes 2097154
  76.8 16.3 %all-to-all-done = bf16[8,2,32768]{2,1,0:T(2,128)(2,1)} async-done(((bf16[8,2,32768]{2,1,0:T(2,128)(2,1)}), bf16[8,2,32768]{2,1,0:T(2,128)(2,1)}, u32[]{:S(2)}, u32[]{:S(2)}) %all-to-all-start) | async-done | bytes 1048608 | tf_op jit(solution)/shard_map/all_to_all | solution.py:113
  93.1 7.5 %all-to-all-start.1 = ((bf16[8,2,32768]{2,1,0:T(2,128)(2,1)}), bf16[8,2,32768]{2,1,0:T(2,128)(2,1)}, u32[]{:S(2)}, u32[]{:S(2)}) async-start(bf16[8,2,32768]{2,1,0:T(2,128)(2,1)} %reshape.236), calls=%async_computation.1 | async-start | bytes 2097152 | tf_op jit(solution)/shard_map/all_to_all | solution.py:114
  100.6 5.0 copy.136
  105.7 23.4 %reduce.10 = bf16[4096,128]{1,0:T(8,128)(2,1)} reduce(bf16[4096,1,128]{2,1,0:T(2,128)(2,1)S(1)} %bitcast.144, bf16[]{:T(256)} %broadcast.182), dimensions={1}, to_apply=%bitcast.92.reduce_sub_computation | reduce | bytes 2097154
  139.8 5.3 all-to-all-start.2
  153.2 5.2 fusion.54
  158.4 103.3 %all-gather.3.cloned.1.call-done = bf16[64,128,2048]{2,1,0:T(8,128)(2,1)} async-done(((bf16[2,128,2048]{2,1,0:T(8,128)(2,1)}), bf16[64,128,2048]{2,1,0:T(8,128)(2,1)}) %all-gather.3.cloned.1.call-update) | async-done | bytes 33554448 | tf_op jit(solution)/shard_map/all_gather | solution.py:124
  261.7 23.6 %fusion.53 = (bf16[1,32,128,2048]{3,2,0,1:T(8,128)(2,1)}, bf16[1,32,128,2048]{3,2,0,1:T(8,128)(2,1)}) fusion(bf16[2,32,128,2048]{3,2,0,1:T(8,128)(2,1)} %bitcast.126), kind=kLoop, calls=%fused_computation.70 | loop fusion | bytes 67108864 | tf_op jit(solution)/shard_map/slice | solution.py:125
  285.3 11.4 %fusion.19 = bf16[128,4096]{1,0:T(8,128)(2,1)S(1)} fusion(bf16[4096,2048]{1,0:T(8,128)(2,1)} %bitcast.122, bf16[1,128,2048]{2,1,0:T(8,128)(2,1)S(1)} %copy-done), kind=kOutput, calls=%fused_computation.40 | convolution fusion | flops 2147483648 | bytes 18350080 | tf_op jit(solution)/shard_map/dot_general | solution.py:92
  296.7 12.4 %fusion.4 = bf16[1,128,4096]{2,1,0:T(8,128)(2,1)} fusion(bf16[128,4096]{1,0:T(8,128)(2,1)S(1)} %fusion.19, bf16[4096,2048]{1,0:T(8,128)(2,1)} %bitcast.124, pred[128]{0:T(512)(128)(4,1)S(1)} %compare_bitcast_fusion, bf16[1,128,2048]{2,1,0:T(8,128)(2,1)S(1)} %copy-done), kind=kOutput, calls=%fused_computation.8 | convolution fusion | flops 2148007936 | bytes 19398784 | tf_op jit(solution)/shard_map/dot_general | solution.py:92
  309.1 5.0 copy.143
  314.1 23.5 %reduce.11 = bf16[4096,128]{1,0:T(8,128)(2,1)} reduce(bf16[4096,1,128]{2,1,0:T(2,128)(2,1)S(1)} %bitcast.139, bf16[]{:T(256)} %broadcast.182), dimensions={1}, to_apply=%bitcast.96.reduce_sub_computation | reduce | bytes 2097154
  344.0 5.3 fusion.8
  370.5 5.8 %reshape.243 = bf16[4096,1,128]{2,1,0:T(2,128)(2,1)} reshape(bf16[8,2,32768]{2,1,0:T(2,128)(2,1)} %all-to-all-done.4) | data formatting | bytes 2097152
  392.4 6.1 %copy.141 = bf16[1,1024,512]{2,0,1:T(2,128)(2,1)} copy(bf16[1,1024,512]{1,2,0:T(8,128)(2,1)} %bitcast.153) | data formatting | bytes 2097152 | tf_op jit(solution)/shard_map/reshape | solution.py:102
  398.5 9.0 %reduce.12 = bf16[1024,512]{1,0:T(8,128)(2,1)} reduce(bf16[1024,1,512]{2,1,0:T(2,128)(2,1)} %bitcast.140, bf16[]{:T(256)} %broadcast.182), dimensions={1}, to_apply=%bitcast.94.reduce_sub_computation | reduce | bytes 2097154
  416.7 5.5 multiply_convert_fusion
  424.5 6.0 %copy.154 = bf16[1,1024,512]{2,0,1:T(2,128)(2,1)} copy(bf16[1,1024,512]{1,2,0:T(8,128)(2,1)} %bitcast.162) | data formatting | bytes 2097152 | tf_op jit(solution)/shard_map/reshape | solution.py:102
  430.5 9.0 %reduce.14 = bf16[1024,512]{1,0:T(8,128)(2,1)} reduce(bf16[1024,1,512]{2,1,0:T(2,128)(2,1)} %bitcast.141, bf16[]{:T(256)} %broadcast.182), dimensions={1}, to_apply=%bitcast.100.reduce_sub_computation | reduce | bytes 2097154
  442.1 6.2 %all-to-all-start.6 = ((bf16[8,2,32768]{2,1,0:T(2,128)(2,1)}), bf16[8,2,32768]{2,1,0:T(2,128)(2,1)}, u32[]{:S(2)}, u32[]{:S(2)}) async-start(bf16[8,2,32768]{2,1,0:T(2,128)(2,1)} %reshape.246), calls=%async_computation.6 | async-start | bytes 2097152 | tf_op jit(solution)/shard_map/all_to_all | solution.py:142
  458.6 9.2 %reduce.13 = bf16[1024,512]{1,0:T(8,128)(2,1)} reduce(bf16[1024,1,512]{2,1,0:T(2,128)(2,1)} %bitcast.142, bf16[]{:T(256)} %broadcast.182), dimensions={1}, to_apply=%bitcast.98.reduce_sub_computation | reduce | bytes 2097154
  489.0 8.0 %reduce.15 = bf16[1024,512]{1,0:T(8,128)(2,1)} reduce(bf16[1024,1,512]{2,1,0:T(2,128)(2,1)S(1)} %bitcast.138, bf16[]{:T(256)} %broadcast.182), dimensions={1}, to_apply=%bitcast.102.reduce_sub_computation | reduce | bytes 2097154
  506.8 5.8 %reshape.247 = bf16[1024,1,512]{2,1,0:T(2,128)(2,1)} reshape(bf16[8,2,32768]{2,1,0:T(2,128)(2,1)} %all-to-all-done.6) | data formatting | bytes 2097152
  518.0 6.3 %all-to-all-start.7 = ((bf16[8,2,32768]{2,1,0:T(2,128)(2,1)}), bf16[8,2,32768]{2,1,0:T(2,128)(2,1)}, u32[]{:S(2)}, u32[]{:S(2)}) async-start(bf16[8,2,32768]{2,1,0:T(2,128)(2,1)} %reshape.248), calls=%async_computation.7 | async-start | bytes 2097152 | tf_op jit(solution)/shard_map/all_to_all | solution.py:145
  524.3 5.8 %reshape.245 = bf16[1024,1,512]{2,1,0:T(2,128)(2,1)} reshape(bf16[8,2,32768]{2,1,0:T(2,128)(2,1)} %all-to-all-done.5) | data formatting | bytes 2097152
  535.5 8.1 %fusion.64 = bf16[128,2048]{1,0:T(8,128)(2,1)S(1)} fusion(bf16[128,4096]{0,1:T(8,128)(2,1)S(1)} %bitcast.127, bf16[4096,2048]{1,0:T(8,128)(2,1)} %bitcast.123), kind=kOutput, calls=%fused_computation.73 | convolution fusion | flops 2147483648 | bytes 18350080 | tf_op jit(solution)/shard_map/dot_general | solution.py:126
  543.7 8.9 %fusion.11 = bf16[1,128,2048]{2,1,0:T(8,128)(2,1)} fusion(bf16[128,2048]{1,0:T(8,128)(2,1)S(1)} %fusion.64, bf16[128,4096]{0,1:T(8,128)(2,1)S(1)} %bitcast.128, bf16[4096,2048]{1,0:T(8,128)(2,1)} %bitcast.125, pred[128]{0:T(512)(128)(4,1)S(1)} %compare_bitcast_fusion), kind=kOutput, calls=%fused_computation.20 | convolution fusion | flops 2147745792 | bytes 18874496 | tf_op jit(solution)/shard_map/dot_general | solution.py:125
  (105 shorter events, 142.4 us)
Async XLA Ops:
  7.2 278.2 %copy-start = (bf16[1,128,2048]{2,1,0:T(8,128)(2,1)S(1)}, bf16[1,128,2048]{2,1,0:T(8,128)(2,1)}, u32[]{:S(2)}) copy-start(bf16[1,128,2048]{2,1,0:T(8,128)(2,1)} %param.23) | copy-start | bytes 1572868
  7.2 254.5 %all-gather.3.cloned.1.call-start = ((), (), s32[]{:S(2)}) async-start(), calls=%async_computation.8 | async-start | bytes 34603008 | tf_op jit(solution)/shard_map/all_gather | solution.py:124
  39.0 54.1 %all-to-all-start = ((bf16[8,2,32768]{2,1,0:T(2,128)(2,1)}), bf16[8,2,32768]{2,1,0:T(2,128)(2,1)}, u32[]{:S(2)}, u32[]{:S(2)}) async-start(bf16[8,2,32768]{2,1,0:T(2,128)(2,1)} %reshape.234), calls=%async_computation | async-start | bytes 2097152 | tf_op jit(solution)/shard_map/all_to_all | solution.py:113
  93.1 46.7 %all-to-all-start.1 = ((bf16[8,2,32768]{2,1,0:T(2,128)(2,1)}), bf16[8,2,32768]{2,1,0:T(2,128)(2,1)}, u32[]{:S(2)}, u32[]{:S(2)}) async-start(bf16[8,2,32768]{2,1,0:T(2,128)(2,1)} %reshape.236), calls=%async_computation.1 | async-start | bytes 2097152 | tf_op jit(solution)/shard_map/all_to_all | solution.py:114
  100.6 30.7 %copy-start.14 = (s32[1,128]{1,0:T(1,128)S(1)}, s32[1,128]{1,0:T(1,128)}, u32[]{:S(2)}) copy-start(s32[1,128]{1,0:T(1,128)} %param.21) | copy-start | bytes 1540
  139.8 200.0 %all-to-all-start.2 = ((bf16[8,2,32768]{2,1,0:T(2,128)(2,1)}), bf16[8,2,32768]{2,1,0:T(2,128)(2,1)}, u32[]{:S(2)}, u32[]{:S(2)}) async-start(bf16[8,2,32768]{2,1,0:T(2,128)(2,1)} %reshape.238), calls=%async_computation.2 | async-start | bytes 2097152 | tf_op jit(solution)/shard_map/all_to_all | solution.py:115
  149.6 3.6 copy-start.5
  153.2 5.2 copy-start.10
  339.8 30.7 %all-to-all-start.4 = ((bf16[8,2,32768]{2,1,0:T(2,128)(2,1)}), bf16[8,2,32768]{2,1,0:T(2,128)(2,1)}, u32[]{:S(2)}, u32[]{:S(2)}) async-start(bf16[8,2,32768]{2,1,0:T(2,128)(2,1)} %reshape.242), calls=%async_computation.4 | async-start | bytes 2097152 | tf_op jit(solution)/shard_map/all_to_all | solution.py:133
  353.9 6.2 %copy-start.6 = (bf16[1024,4,128]{2,0,1:T(8,128)(2,1)S(1)}, bf16[1024,4,128]{2,0,1:T(8,128)(2,1)}, u32[]{:S(2)}) copy-start(bf16[1024,4,128]{2,0,1:T(8,128)(2,1)} %copy.132) | copy-start | bytes 3145732
  353.9 6.2 %copy-start.11 = (bf16[1024,4,128]{2,0,1:T(8,128)(2,1)S(1)}, bf16[1024,4,128]{2,0,1:T(8,128)(2,1)}, u32[]{:S(2)}) copy-start(bf16[1024,4,128]{2,0,1:T(8,128)(2,1)} %copy-done.10) | copy-start | bytes 3145732
  360.1 2.2 copy-start.2
  360.1 2.5 copy-start.13
  366.0 2.0 copy-start.8
  368.6 15.7 %copy-start.3 = (bf16[4,512,512]{1,2,0:T(8,128)(2,1)}, bf16[4,512,512]{1,2,0:T(8,128)(2,1)S(1)}, u32[]{:S(2)}) copy-start(bf16[4,512,512]{1,2,0:T(8,128)(2,1)S(1)} %fusion.15) | copy-start | bytes 6291460
  384.2 2.8 copy-start.9
  410.2 31.9 %all-to-all-start.3 = ((bf16[8,2,32768]{2,1,0:T(2,128)(2,1)}), bf16[8,2,32768]{2,1,0:T(2,128)(2,1)}, u32[]{:S(2)}, u32[]{:S(2)}) async-start(bf16[8,2,32768]{2,1,0:T(2,128)(2,1)} %reshape.240), calls=%async_computation.3 | async-start | bytes 2097152 | tf_op jit(solution)/shard_map/all_to_all | solution.py:122
  416.7 5.5 copy-start.7
  422.2 2.3 copy-start.12
  442.1 31.8 %all-to-all-start.6 = ((bf16[8,2,32768]{2,1,0:T(2,128)(2,1)}), bf16[8,2,32768]{2,1,0:T(2,128)(2,1)}, u32[]{:S(2)}, u32[]{:S(2)}) async-start(bf16[8,2,32768]{2,1,0:T(2,128)(2,1)} %reshape.246), calls=%async_computation.6 | async-start | bytes 2097152 | tf_op jit(solution)/shard_map/all_to_all | solution.py:142
  458.6 19.8 %copy-start.4 = (bf16[4,512,512]{1,2,0:T(8,128)(2,1)S(1)}, bf16[4,512,512]{1,2,0:T(8,128)(2,1)}, u32[]{:S(2)}) copy-start(bf16[4,512,512]{1,2,0:T(8,128)(2,1)} %copy-done.3) | copy-start | bytes 6291460
  473.9 44.1 %all-to-all-start.5 = ((bf16[8,2,32768]{2,1,0:T(2,128)(2,1)}), bf16[8,2,32768]{2,1,0:T(2,128)(2,1)}, u32[]{:S(2)}, u32[]{:S(2)}) async-start(bf16[8,2,32768]{2,1,0:T(2,128)(2,1)} %reshape.244), calls=%async_computation.5 | async-start | bytes 2097152 | tf_op jit(solution)/shard_map/all_to_all | solution.py:139
  518.0 34.6 %all-to-all-start.7 = ((bf16[8,2,32768]{2,1,0:T(2,128)(2,1)}), bf16[8,2,32768]{2,1,0:T(2,128)(2,1)}, u32[]{:S(2)}, u32[]{:S(2)}) async-start(bf16[8,2,32768]{2,1,0:T(2,128)(2,1)} %reshape.248), calls=%async_computation.7 | async-start | bytes 2097152 | tf_op jit(solution)/shard_map/all_to_all | solution.py:145
  552.6 8.6 %copy-start.1 = (bf16[1,128,2048]{2,1,0:T(8,128)(2,1)S(1)}, bf16[1,128,2048]{2,1,0:T(8,128)(2,1)}, u32[]{:S(2)}) copy-start(bf16[1,128,2048]{2,1,0:T(8,128)(2,1)} %param.23) | copy-start | bytes 1572868
Sparse Core Ops, SparseCore 0:
  11.0 250.6 all-gather.2
